TPU v7x, 256 devices: a whole 4x4x8 slice. The times are simulated.
256 devices in a mesh: group: 32 (over x, z), span: 8 (over y, core).
Axes of the slice: x: 4, y: 4, z: 8, core: 2. Of those that a mesh axis runs over, the one named last changes fastest.
Arguments:
- struct_disp: float32 [3, 524288], P(None, ('group', 'span')), may hold values from -6 to 6
- interp_weight: float32 [524288, 4], P(('group', 'span')), may hold values from 0.2 to 1
- face_owner: int32 [524288, 4], P(('group', 'span')), may hold values from 0 to 31, all different within a row; in each aligned block of 2048 rows (0 to 2047, 2048 to 4095, ...) at most 512 rows name the same one
- face_row: int32 [524288, 4], P(('group', 'span')), may hold values from 0 to 20479
- skel_force: float32 [3, 16384], P(None, ('group', 'span')), may hold values from -6 to 6
- skel_coupling: float32 [6, 16384], P(None, ('group', 'span')), may hold values from 0.1 to 0.2
- skel_stiff: float32 [16384], P(('group', 'span')), may hold values from 0.05 to 0.15
- skel_edges: int32 [6, 16384], P(None, ('group', 'span')), may hold values from 0 to 16383
- block_spacing: float32 [3, 256], P(None, 'group'), may hold values from 1 to 2
Outputs:
- displacement: float32 [3, 256, 64, 6400], P(None, 'group', 'span')
- jacobian: float32 [256, 64, 6400], P('group', 'span')
Inputs may be any that keep to these rules, and one draw needn't show every extreme that they name: `face_owner`: each row names 4 different group indices; among the rows of one device no index is named more than 512 times, a bound that some block reaches.
All inputs are finite; a program needn't handle non-finite values.
Results may differ from a plain program's by a relative error of at most 0.0001.
Values sent between devices are 32-bit elements; how exact they have to be, the bound alone decides.
A program may use at most 128 MiB of HBM per device.

v0:
```python
import jax
import jax.numpy as jnp
from jax import lax
from jax.sharding import PartitionSpec as P

BPD = 8
SPAN_DEV = 8
NP = 80
ITERS = 4


def with_halo(block, sides, width):
    for axis, dim in sides:
        count = lax.axis_size(axis)
        forward = [(i, i + 1) for i in range(count - 1)]
        backward = [(target, source) for source, target in forward]
        low = lax.ppermute(
            lax.slice_in_dim(block, block.shape[dim] - width, None, axis=dim), axis, forward
        )
        high = lax.ppermute(lax.slice_in_dim(block, 0, width, axis=dim), axis, backward)
        block = jnp.concatenate([low, block, high], axis=dim)
    return block


def tfi_tables(points):
    position = jnp.arange(points * points, dtype=jnp.int32)
    first = position % points
    second = position // points
    frac_first = first.astype(jnp.float32) / (points - 1)
    frac_second = second.astype(jnp.float32) / (points - 1)
    edge_pos = jnp.arange(points, dtype=jnp.int32)[:, None]
    zero = jnp.zeros((points, points * points), jnp.float32)
    bottom = jnp.where(first[None] == edge_pos, (1.0 - frac_second)[None], zero)
    bottom = bottom.at[0].add(-(1.0 - frac_first) * (1.0 - frac_second))
    bottom = bottom.at[points - 1].add(-frac_first * (1.0 - frac_second))
    top_rows = jnp.where(first[None] == edge_pos, frac_second[None], zero)
    top_rows = top_rows.at[0].add(-(1.0 - frac_first) * frac_second)
    top_rows = top_rows.at[points - 1].add(-frac_first * frac_second)
    left_rows = jnp.where(second[None] == edge_pos, (1.0 - frac_first)[None], zero)
    right_rows = jnp.where(second[None] == edge_pos, frac_first[None], zero)
    table = jnp.concatenate([bottom, top_rows, left_rows, right_rows], axis=0)
    bubble = 16.0 * frac_first * (1.0 - frac_first) * frac_second * (1.0 - frac_second)
    return (table, bubble)


def plane_derivs(field, points):
    position = jnp.arange(points * points, dtype=jnp.int32)
    first = position % points
    second = position // points
    ahead = jnp.concatenate([field[..., 1:], field[..., -1:]], axis=-1)
    behind = jnp.concatenate([field[..., :1], field[..., :-1]], axis=-1)
    deriv_first = (
        jnp.where(first == points - 1, field, ahead) - jnp.where(first == 0, field, behind)
    ) * 0.5
    upper = jnp.concatenate([field[..., points:], field[..., -points:]], axis=-1)
    lower = jnp.concatenate([field[..., :points], field[..., :-points]], axis=-1)
    deriv_second = (
        jnp.where(second == points - 1, field, upper) - jnp.where(second == 0, field, lower)
    ) * 0.5
    return (deriv_first, deriv_second)


def metric_det(spacing, deriv_first, deriv_second, deriv_span):
    derivs = (deriv_first, deriv_second, deriv_span)
    matrix = [[derivs[col][row] for col in range(3)] for row in range(3)]
    for row in range(3):
        matrix[row][row] = matrix[row][row] + spacing[row][:, None, None]
    minor_one = matrix[1][1] * matrix[2][2] - matrix[1][2] * matrix[2][1]
    minor_two = matrix[1][0] * matrix[2][2] - matrix[1][2] * matrix[2][0]
    minor_three = matrix[1][0] * matrix[2][1] - matrix[1][1] * matrix[2][0]
    return matrix[0][0] * minor_one - matrix[0][1] * minor_two + matrix[0][2] * minor_three


def blend_layers(faces, skel_values, table, bubble):
    blended = jnp.dot(
        faces.reshape(-1, faces.shape[-1]),
        table,
        precision=lax.Precision.HIGHEST,
        preferred_element_type=jnp.float32,
    )
    shape = faces.shape[:-1] + (bubble.shape[0],)
    return blended.reshape(shape) + skel_values * bubble


def on_device(
    struct_disp,
    interp_weight,
    face_owner,
    face_row,
    skel_force,
    skel_coupling,
    skel_stiff,
    skel_edges,
    block_spacing,
):
    group_count = lax.axis_size("group")
    local_nodes = skel_force.shape[1]
    face_total = BPD * SPAN_DEV * 4 * NP
    weighted = (struct_disp[:, :, None] * interp_weight[None]).reshape(3, -1)
    owners = face_owner.reshape(-1)
    targets = face_row.reshape(-1)
    empty_faces = jnp.zeros((3, face_total), jnp.float32)
    contributions = owners.shape[0]
    capacity = 2 * contributions // group_count
    one_hot = (owners[:, None] == jnp.arange(group_count, dtype=jnp.int32)[None]).astype(jnp.int32)
    running = jnp.cumsum(one_hot, axis=0)
    slot_index = jnp.sum((running - 1) * one_hot, axis=1)
    send_values = (
        jnp.zeros((group_count, 3, capacity), jnp.float32).at[owners, :, slot_index].set(weighted.T)
    )
    send_rows = jnp.zeros((group_count, capacity), jnp.int32).at[owners, slot_index].set(targets)
    recv_values, recv_rows = (
        lax.all_to_all(send_values, "group", split_axis=0, concat_axis=0, tiled=True),
        lax.all_to_all(send_rows, "group", split_axis=0, concat_axis=0, tiled=True),
    )
    face_disp = empty_faces.at[:, recv_rows.reshape(-1)].add(
        recv_values.transpose(1, 0, 2).reshape(3, -1)
    )
    face_disp = face_disp.reshape(3, BPD, SPAN_DEV, 4 * NP)
    skeleton_rhs = skel_force + (0.25 * jnp.sum(face_disp, axis=3)).reshape(3, local_nodes)
    diagonal = skel_stiff + jnp.sum(skel_coupling, axis=0)

    def sweep(sweep_index, state):
        whole_state = lax.all_gather(state, ("group", "span"), axis=1, tiled=True)
        neighbours = whole_state[:, skel_edges]
        return (skeleton_rhs + jnp.sum(skel_coupling[None] * neighbours, axis=1)) / diagonal

    skeleton = lax.fori_loop(0, ITERS, sweep, jnp.zeros((3, local_nodes), jnp.float32))
    table, bubble = tfi_tables(NP)
    skel_layers = skeleton.reshape(3, BPD, SPAN_DEV, 1)
    displacement = blend_layers(face_disp, skel_layers, table, bubble)
    deriv_first, deriv_second = plane_derivs(displacement, NP)
    padded = with_halo(displacement, (("span", 2),), 1)
    deriv_span = (padded[:, :, 2:] - padded[:, :, :-2]) * 0.5
    jacobian = metric_det(block_spacing, deriv_first, deriv_second, deriv_span)
    return (displacement, jacobian)


def solution(mesh):
    return jax.shard_map(
        on_device,
        mesh=mesh,
        in_specs=(
            P(None, ("group", "span")),
            P(("group", "span"), None),
            P(("group", "span"), None),
            P(("group", "span"), None),
            P(None, ("group", "span")),
            P(None, ("group", "span")),
            P(("group", "span")),
            P(None, ("group", "span")),
            P(None, "group"),
        ),
        out_specs=(P(None, "group", "span", None), P("group", "span", None)),
        check_vma=False,
    )
```

profile of v0, /device:TPU:1, one launch (start us, length us, event | category | flops | bytes accessed | tf_op | source)
XLA Modules:
  0.0 607.1 jit_solution(6317149871625907783)
XLA Ops:
  3.9 9.5 %reduce-window.6 = s32[32,64,128]{2,1,0:T(8,128)S(1)} reduce-window(s32[32,64,128]{2,1,0:T(8,128)S(1)} %fusion.34, s32[]{:T(128)} %constant.154.clone.1), window={size=1x1x128 pad=0_0x0_0x127_0}, to_apply=%region_0.0 | reduce-window | flops 33292288 | bytes 2097156 | tf_op jit(solution)/shard_map/reduce-window
  17.2 31.0 %scatter_custom_fusion.1 = s32[16384]{0:T(1024)} fusion(s32[8192]{0:T(1024)S(1)} %broadcast_select_fusion, s32[8192]{0:T(1024)S(1)} %reshape.387, s32[]{:T(128)} %constant.154.clone.1), kind=kCustom, calls=%fused_computation.84 | custom fusion | bytes 65540
  48.2 11.9 %all-to-all-start = ((s32[32,1,512]{2,1,0:T(1,128)}), s32[32,1,512]{2,1,0:T(1,128)S(1)}, u32[]{:S(2)}, u32[]{:S(2)}) async-start(s32[32,1,512]{2,1,0:T(1,128)} %bitcast.2), calls=%async_computation | async-start | bytes 131072 | tf_op jit(solution)/shard_map/all_to_all | solution.py:114
  72.1 28.8 %scatter_custom_fusion.2 = f32[3,16384]{0,1:T(8,128)} fusion(s32[8192]{0:T(1024)S(1)} %broadcast_select_fusion, f32[]{:T(128)} %constant.153.clone.1, f32[3,8192]{0,1:T(8,128)} %bitcast.125, f32[8192]{0:T(1024)S(1)} %mul.156), kind=kCustom, calls=%fused_computation.32 | custom fusion | flops 24576 | bytes 327684
  101.0 6.1 copy.42
  109.5 9.2 %all-to-all-start.1 = ((f32[32,3,512]{2,1,0:T(4,128)}), f32[32,3,512]{2,1,0:T(4,128)S(1)}, u32[]{:S(2)}, u32[]{:S(2)}) async-start(f32[32,3,512]{2,1,0:T(4,128)} %bitcast.8), calls=%async_computation.1 | async-start | bytes 524288 | tf_op jit(solution)/shard_map/all_to_all | solution.py:113
  118.8 9.6 %all-to-all-done.1 = f32[32,3,512]{2,1,0:T(4,128)S(1)} async-done(((f32[32,3,512]{2,1,0:T(4,128)}), f32[32,3,512]{2,1,0:T(4,128)S(1)}, u32[]{:S(2)}, u32[]{:S(2)}) %all-to-all-start.1) | async-done | bytes 196640 | tf_op jit(solution)/shard_map/all_to_all | solution.py:113
  128.4 5.1 copy.43
  133.5 102.3 %scatter_custom_fusion = f32[3,20480]{0,1:T(8,128)} fusion(s32[16384]{0:T(1024)S(1)} %bitcast.133, f32[16384,3]{1,0:T(8,128)} %copy.43, f32[]{:T(128)} %constant.153.clone.1), kind=kCustom, calls=%fused_computation.18 | custom fusion | flops 49152 | bytes 246272 | tf_op jit(solution)/shard_map/scatter-add | solution.py:116
  235.8 6.4 %copy.44 = f32[3,8,8,320]{3,2,1,0:T(8,128)S(1)} copy(f32[3,8,8,320]{0,3,2,1:T(8,128)} %bitcast.122) | data formatting | bytes 491520 | tf_op jit(solution)/shard_map/dot_general | solution.py:75
  242.2 5.4 reduce_sum.40
  247.6 315.2 %while.15 = (s32[]{:T(128)}, f32[3,64]{0,1:T(8,128)S(1)}, f32[6,64]{1,0:T(8,128)S(1)}, s32[6,64]{1,0:T(8,128)S(1)}, f32[3,64]{0,1:T(8,128)S(1)}, /*index=5*/f32[64]{0:T(128)S(1)}, s32[]{:T(128)}, s32[]{:T(128)}) while((s32[]{:T(128)}, f32[3,64]{0,1:T(8,128)S(1)}, f32[6,64]{1,0:T(8,128)S(1)}, s32[6,64]{1,0:T(8,128)S(1)}, ...), condition=%wide.region_10.11_spmd.clone, body=%wide.region_8.0_spmd.clone.sunk | while | flops 4867 | bytes 625759 | solution.py:128
  247.7 79.7 %all-gather.3 = f32[256,64,3]{1,2,0:T(4,128)S(1)} all-gather(f32[1,64,3]{1,2,0:T(4,128)S(1)} %select_bitcast_fusion.2), channel_id=1, replica_groups=mesh['group'=32,'span'=8] {'group','span'}, dimensions={0}, use_global_device_ids=true | all-gather | bytes 197376 | tf_op jit(solution)/shard_map/while/body/eval_jaxpr/all_gather | solution.py:124
  327.4 4.8 copy.53
  337.1 65.6 %all-gather.3 = f32[256,64,3]{1,2,0:T(4,128)S(1)} all-gather(f32[1,64,3]{1,2,0:T(4,128)S(1)} %select_bitcast_fusion.2), channel_id=1, replica_groups=mesh['group'=32,'span'=8] {'group','span'}, dimensions={0}, use_global_device_ids=true | all-gather | bytes 197376 | tf_op jit(solution)/shard_map/while/body/eval_jaxpr/all_gather | solution.py:124
  402.7 4.8 copy.53
  412.4 65.6 %all-gather.3 = f32[256,64,3]{1,2,0:T(4,128)S(1)} all-gather(f32[1,64,3]{1,2,0:T(4,128)S(1)} %select_bitcast_fusion.2), channel_id=1, replica_groups=mesh['group'=32,'span'=8] {'group','span'}, dimensions={0}, use_global_device_ids=true | all-gather | bytes 197376 | tf_op jit(solution)/shard_map/while/body/eval_jaxpr/all_gather | solution.py:124
  478.0 4.8 copy.53
  487.7 65.6 %all-gather.3 = f32[256,64,3]{1,2,0:T(4,128)S(1)} all-gather(f32[1,64,3]{1,2,0:T(4,128)S(1)} %select_bitcast_fusion.2), channel_id=1, replica_groups=mesh['group'=32,'span'=8] {'group','span'}, dimensions={0}, use_global_device_ids=true | all-gather | bytes 197376 | tf_op jit(solution)/shard_map/while/body/eval_jaxpr/all_gather | solution.py:124
  553.3 4.8 copy.53
  563.0 10.6 %convolution_add_fusion = f32[3,8,8,6400]{3,2,1,0:T(8,128)S(1)} fusion(f32[3,8,8,320]{3,2,1,0:T(8,128)S(1)} %copy.44, f32[80,6400]{1,0:T(8,128)} %get-tuple-element.132, f32[80,6400]{1,0:T(8,128)} %get-tuple-element.131, f32[80,6400]{1,0:T(8,128)S(1)} %scatter-add.31, f32[80,6400]{1,0:T(8,128)} %scatter-add.24, f32[6400]{0:T(1024)S(1)} %multiply_multiply_fusion, ...), kind=kOutput, calls=%fused_computation.10 | convolution fusion | flops 4727193600 | bytes 13379328 | tf_op jit(solution)/shard_map/dot_general | solution.py:75
  573.6 5.3 fusion.48
  585.6 5.5 fusion.50
  592.4 10.9 %fusion.12 = (f32[3,8,8,6400]{3,2,1,0:T(8,128)S(1)}, f32[3,8,8,6400]{3,2,1,0:T(8,128)S(1)}, f32[3,8,8,6400]{3,2,1,0:T(8,128)}) fusion(f32[3,8,8,6400]{3,2,1,0:T(8,128)S(1)} %convolution_add_fusion, f32[3,8,8,1]{3,2,1,0:T(8,128)S(1)} %get-tuple-element.120, f32[3,8,8,6399]{3,2,1,0:T(8,128)} %get-tuple-element.122, f32[3,8,8,6399]{3,2,1,0:T(8,128)} %get-tuple-element.121, ...), kind=kLoop, calls=%fused_computation.26 | loop fusion | flops 19660800 | bytes 40576000 | tf_op jit(solution)/shard_map/mul | solution.py:52
  (113 shorter events, 52.6 us)
Async XLA Ops:
  2.4 13.4 %copy-start.12 = (s32[2]{0:T(128)S(1)}, s32[2]{0:T(128)}, u32[]{:S(2)}) copy-start(s32[2]{0:T(128)} %constant.172) | copy-start | bytes 28
  2.4 13.6 %copy-start.11 = (s32[2]{0:T(128)S(1)}, s32[2]{0:T(128)}, u32[]{:S(2)}) copy-start(s32[2]{0:T(128)} %constant.175) | copy-start | bytes 28
  2.4 13.7 %copy-start.6 = (s32[2048,4]{0,1:T(4,128)S(1)}, s32[2048,4]{0,1:T(4,128)}, u32[]{:S(2)}) copy-start(s32[2048,4]{0,1:T(4,128)} %param.22) | copy-start | bytes 98308
  14.6 51.1 %copy-start.10 = (f32[3,8]{1,0:T(4,128)S(1)}, f32[3,8]{1,0:T(4,128)}, u32[]{:S(2)}) copy-start(f32[3,8]{1,0:T(4,128)} %param.27) | copy-start | bytes 292
  16.5 51.8 %copy-start.7 = (f32[3,2048]{1,0:T(4,128)S(1)}, f32[3,2048]{1,0:T(4,128)}, u32[]{:S(2)}) copy-start(f32[3,2048]{1,0:T(4,128)} %param.19) | copy-start | bytes 73732
  48.2 61.3 %all-to-all-start = ((s32[32,1,512]{2,1,0:T(1,128)}), s32[32,1,512]{2,1,0:T(1,128)S(1)}, u32[]{:S(2)}, u32[]{:S(2)}) async-start(s32[32,1,512]{2,1,0:T(1,128)} %bitcast.2), calls=%async_computation | async-start | bytes 131072 | tf_op jit(solution)/shard_map/all_to_all | solution.py:114
  60.2 8.5 %copy-start.8 = (f32[2048,4]{0,1:T(4,128)S(1)}, f32[2048,4]{0,1:T(4,128)}, u32[]{:S(2)}) copy-start(f32[2048,4]{0,1:T(4,128)} %param.20) | copy-start | bytes 98308
  60.5 1.3 copy-start.3
  65.6 2.8 copy-start.1
  101.0 6.1 %copy-start.9 = (f32[3,64]{1,0:T(4,128)S(1)}, f32[3,64]{1,0:T(4,128)}, u32[]{:S(2)}) copy-start(f32[3,64]{1,0:T(4,128)} %param.23) | copy-start | bytes 2308
  101.0 6.2 %copy-start.4 = (f32[6,64]{1,0:T(8,128)S(1)}, f32[6,64]{1,0:T(8,128)}, u32[]{:S(2)}) copy-start(f32[6,64]{1,0:T(8,128)} %param.24) | copy-start | bytes 4612
  101.0 7.9 %copy-start.2 = (f32[80,6400]{1,0:T(8,128)S(1)}, f32[80,6400]{1,0:T(8,128)}, u32[]{:S(2)}) copy-start(f32[80,6400]{1,0:T(8,128)} %copy-done.1) | copy-start | bytes 6144004
  101.0 8.5 %copy-start.13 = (f32[64]{0:T(128)S(1)}, f32[64]{0:T(128)}, u32[]{:S(2)}) copy-start(f32[64]{0:T(128)} %param.25) | copy-start | bytes 772
  109.5 18.9 %all-to-all-start.1 = ((f32[32,3,512]{2,1,0:T(4,128)}), f32[32,3,512]{2,1,0:T(4,128)S(1)}, u32[]{:S(2)}, u32[]{:S(2)}) async-start(f32[32,3,512]{2,1,0:T(4,128)} %bitcast.8), calls=%async_computation.1 | async-start | bytes 524288 | tf_op jit(solution)/shard_map/all_to_all | solution.py:113
  242.2 5.4 copy-start.5
  573.6 18.7 %copy-start = (f32[3,8,8,6400]{3,2,1,0:T(8,128)}, f32[3,8,8,6400]{3,2,1,0:T(8,128)S(1)}, u32[]{:S(2)}) copy-start(f32[3,8,8,6400]{3,2,1,0:T(8,128)S(1)} %convolution_add_fusion) | copy-start | bytes 14745604
  579.7 11.5 %collective-permute-start = (f32[3,8,1,6400]{3,2,1,0:T(1,128)S(1)}, f32[3,8,1,6400]{3,2,1,0:T(1,128)S(1)}, u32[]{:S(2)}, u32[]{:S(2)}) collective-permute-start(f32[3,8,1,6400]{3,2,1,0:T(1,128)S(1)} %get-tuple-element.127), channel_id=1, source_target_pairs={{1,0},{2,1},{3,2},{4,3},{5,4},{6,5},{7,6},{9,8},{10,9},{11,10},{12... | collective-permute-start | bytes 1843208 | tf_op jit(solution)/shard_map/ppermute | solution.py:20
  581.8 10.6 %collective-permute-start.1 = (f32[3,8,1,6400]{3,2,1,0:T(1,128)S(1)}, f32[3,8,1,6400]{3,2,1,0:T(1,128)S(1)}, u32[]{:S(2)}, u32[]{:S(2)}) collective-permute-start(f32[3,8,1,6400]{3,2,1,0:T(1,128)S(1)} %get-tuple-element.128), channel_id=1, source_target_pairs={{0,1},{1,2},{2,3},{3,4},{4,5},{5,6},{6,7},{8,9},{9,10},{10,11},{11... | collective-permute-start | bytes 1843208 | tf_op jit(solution)/shard_map/ppermute | solution.py:17
where the time goes:
time: 608 us; the launch traced here: 607 us
  blocking collectives  276 us (45%)
  other arithmetic  168 us (28%)
  local copies, waits for them, and re-layouts  113 us (19%)
  starting transfers between devices  26.9 us (4%)
  waiting for transfers between devices  10.7 us (2%)
  matrix products  10.6 us (2%)
    all_gather x4, blocking collectives, sweep(): whole_state = lax.all_gather(state, ('group', 'span'), axis=1, tiled=True)  276 us
    scatter-add x1, other arithmetic, on_device(): empty_faces.at[:, recv_rows.reshape(-1)]  102 us
    unnamed x35, local copies, waits for them, and re-layouts  40.8 us
    unnamed x5, other arithmetic  29.2 us
    all_gather x4, local copies, waits for them, and re-layouts, sweep(): whole_state = lax.all_gather(state, ('group', 'span'), axis=1, tiled=True)  19.2 us
    gather x4, local copies, waits for them, and re-layouts, sweep(): neighbours = whole_state[:, skel_edges]  18 us
  transfers between devices with their start and end apart: 4, of which 2 were waited for; matrix products, arithmetic and copies ran while one was open for 9% of the time, Pallas kernels for 0%

commit v1 on v0

--- a/solution.py
+++ b/solution.py
@@ -121,7 +121,10 @@
     diagonal = skel_stiff + jnp.sum(skel_coupling, axis=0)
 
     def sweep(sweep_index, state):
-        whole_state = lax.all_gather(state, ("group", "span"), axis=1, tiled=True)
+        size = lax.axis_size(("group", "span"))
+        blocks = jnp.stack([state for _ in range(size)])
+        blocks = lax.all_to_all(blocks, ("group", "span"), split_axis=0, concat_axis=0)
+        whole_state = jnp.concatenate(blocks, axis=1)
         neighbours = whole_state[:, skel_edges]
         return (skeleton_rhs + jnp.sum(skel_coupling[None] * neighbours, axis=1)) / diagonal
 

time: 608 us -> 442 us (0.73)
  blocking collectives: 276 us -> 0 us
  waiting for transfers between devices: 10.7 us -> 72.2 us
  starting transfers between devices: 26.9 us -> 62.7 us
  local copies, waits for them, and re-layouts: 113 us -> 121 us
    all_gather x4 -> x0, blocking collectives: 276 us -> none  [sweep(): whole_state = lax.all_gather(state, ('group', 'span'), axis=1, tiled=True)]
    all_to_all x0 -> x4, waiting for transfers between devices: none -> 61.4 us  [sweep(): lax.all_to_all(blocks, ('group', 'span'), split_axis=0, concat_axis=0)]
    all_to_all x0 -> x4, starting transfers between devices: none -> 35.8 us  [sweep(): lax.all_to_all(blocks, ('group', 'span'), split_axis=0, concat_axis=0)]
    reshape x0 -> x4, local copies, waits for them, and re-layouts: none -> 19.2 us  [sweep(): whole_state = jnp.concatenate(blocks, axis=1)]
    all_gather x4 -> x0, local copies, waits for them, and re-layouts: 19.2 us -> none  [sweep(): whole_state = lax.all_gather(state, ('group', 'span'), axis=1, tiled=True)]
  transfers between devices with their start and end apart: 4 -> 8, of which waited for: 2 -> 6; matrix products, arithmetic and copies ran while one was open for 9% -> 11% of each run, Pallas kernels for 0% -> 0%
where the time goes in v1:
time: 442 us; the launch traced here: 441 us
  other arithmetic  173 us (39%)
  local copies, waits for them, and re-layouts  121 us (27%)
  waiting for transfers between devices  72.2 us (16%)
  starting transfers between devices  62.7 us (14%)
  matrix products  10.6 us (2%)
    scatter-add x1, other arithmetic, on_device(): empty_faces.at[:, recv_rows.reshape(-1)]  102 us
    all_to_all x4, waiting for transfers between devices, sweep(): lax.all_to_all(blocks, ('group', 'span'), split_axis=0, concat_axis=0)  61.4 us
    unnamed x35, local copies, waits for them, and re-layouts  40.8 us
    all_to_all x4, starting transfers between devices, sweep(): lax.all_to_all(blocks, ('group', 'span'), split_axis=0, concat_axis=0)  35.8 us
    unnamed x5, other arithmetic  29.2 us
    reshape x4, local copies, waits for them, and re-layouts, sweep(): whole_state = jnp.concatenate(blocks, axis=1)  19.2 us
    gather x4, local copies, waits for them, and re-layouts, sweep(): neighbours = whole_state[:, skel_edges]  18 us
    all_to_all x1, starting transfers between devices, on_device(): lax.all_to_all(send_rows, 'group', split_axis=0, concat_axis=0, tiled=True)  12 us
  transfers between devices with their start and end apart: 8, of which 6 were waited for; matrix products, arithmetic and copies ran while one was open for 11% of the time, Pallas kernels for 0%

profile of v1, /device:TPU:1, one launch (start us, length us, event | category | flops | bytes accessed | tf_op | source)
XLA Modules:
  0.0 440.6 jit_solution(14900425258373399245)
XLA Ops:
  4.1 9.5 %reduce-window.6 = s32[32,64,128]{2,1,0:T(8,128)S(1)} reduce-window(s32[32,64,128]{2,1,0:T(8,128)S(1)} %fusion.34, s32[]{:T(128)} %constant.154.clone.1), window={size=1x1x128 pad=0_0x0_0x127_0}, to_apply=%region_0.0 | reduce-window | flops 33292288 | bytes 2097156 | tf_op jit(solution)/shard_map/reduce-window
  22.7 31.0 %scatter_custom_fusion.1 = s32[16384]{0:T(1024)} fusion(s32[8192]{0:T(1024)S(1)} %broadcast_select_fusion.1, s32[8192]{0:T(1024)S(1)} %reshape.395, s32[]{:T(128)} %constant.154.clone.1), kind=kCustom, calls=%fused_computation.84 | custom fusion | bytes 65540
  56.0 12.0 %all-to-all-start.1 = ((s32[32,1,512]{2,1,0:T(1,128)}), s32[32,1,512]{2,1,0:T(1,128)S(1)}, u32[]{:S(2)}, u32[]{:S(2)}) async-start(s32[32,1,512]{2,1,0:T(1,128)} %bitcast.2), calls=%async_computation.1 | async-start | bytes 131072 | tf_op jit(solution)/shard_map/all_to_all | solution.py:114
  71.9 28.8 %scatter_custom_fusion.2 = f32[3,16384]{0,1:T(8,128)} fusion(s32[8192]{0:T(1024)S(1)} %broadcast_select_fusion.1, f32[]{:T(128)} %constant.153.clone.1, f32[3,8192]{0,1:T(8,128)} %bitcast.121, f32[8192]{0:T(1024)S(1)} %mul.156), kind=kCustom, calls=%fused_computation.32 | custom fusion | flops 24576 | bytes 327684
  100.7 6.1 %copy.42 = f32[3,32,512]{2,0,1:T(4,128)} copy(f32[3,32,512]{0,2,1:T(8,128)} %bitcast.120) | data formatting | bytes 393216
  109.2 9.1 %all-to-all-start.2 = ((f32[32,3,512]{2,1,0:T(4,128)}), f32[32,3,512]{2,1,0:T(4,128)S(1)}, u32[]{:S(2)}, u32[]{:S(2)}) async-start(f32[32,3,512]{2,1,0:T(4,128)} %bitcast.8), calls=%async_computation.2 | async-start | bytes 524288 | tf_op jit(solution)/shard_map/all_to_all | solution.py:113
  118.4 9.6 %all-to-all-done.2 = f32[32,3,512]{2,1,0:T(4,128)S(1)} async-done(((f32[32,3,512]{2,1,0:T(4,128)}), f32[32,3,512]{2,1,0:T(4,128)S(1)}, u32[]{:S(2)}, u32[]{:S(2)}) %all-to-all-start.2) | async-done | bytes 196640 | tf_op jit(solution)/shard_map/all_to_all | solution.py:113
  128.0 5.1 %copy.43 = f32[16384,3]{1,0:T(8,128)} copy(f32[16384,3]{0,1:T(4,128)S(1)} %bitcast.125) | data formatting | bytes 393216 | tf_op jit(solution)/shard_map/reshape | solution.py:117
  133.0 102.3 %scatter_custom_fusion = f32[3,20480]{0,1:T(8,128)} fusion(s32[16384]{0:T(1024)S(1)} %bitcast.129, f32[16384,3]{1,0:T(8,128)} %copy.43, f32[]{:T(128)} %constant.153.clone.1), kind=kCustom, calls=%fused_computation.18 | custom fusion | flops 49152 | bytes 246272 | tf_op jit(solution)/shard_map/scatter-add | solution.py:116
  235.3 6.4 %copy.44 = f32[3,8,8,320]{3,2,1,0:T(8,128)S(1)} copy(f32[3,8,8,320]{0,3,2,1:T(8,128)} %bitcast.117) | data formatting | bytes 491520 | tf_op jit(solution)/shard_map/dot_general | solution.py:75
  241.8 5.4 %reduce_sum.40 = f32[3,8,8]{0,2,1:T(8,128)S(1)} reduce(f32[3,8,8,320]{0,3,2,1:T(8,128)} %bitcast.118, f32[]{:T(128)} %constant.153.clone.1), dimensions={3}, to_apply=%region_6.7 | reduce | flops 61248 | bytes 246532 | tf_op jit(solution)/shard_map/reduce_sum | solution.py:120
  247.2 149.2 %while.15 = (s32[]{:T(128)}, f32[3,64]{0,1:T(8,128)S(1)}, f32[6,64]{1,0:T(8,128)S(1)}, s32[6,64]{1,0:T(8,128)S(1)}, f32[3,64]{0,1:T(8,128)S(1)}, /*index=5*/f32[64]{0:T(128)S(1)}, s32[]{:T(128)}, s32[]{:T(128)}, f32[]{:T(128)}) while((s32[]{:T(128)}, f32[3,64]{0,1:T(8,128)S(1)}, f32[6,64]{1,0:T(8,128)S(1)}, ...), condition=%wide.region_10.11_spmd.clone, body=%wide.region_8.0_spmd.clone.sunk | while | flops 4867 | bytes 2526355 | solution.py:131
  248.5 20.3 %all-to-all-start = ((f32[256,1,192]{2,1,0:T(1,128)}), f32[256,1,192]{2,1,0:T(1,128)S(1)}, u32[]{:S(2)}, u32[]{:S(2)}) async-start(f32[256,1,192]{2,1,0:T(1,128)} %reshape.430), calls=%async_computation | async-start | bytes 524288 | tf_op jit(solution)/shard_map/while/body/eval_jaxpr/all_to_all | solution.py:126
  269.0 15.4 %all-to-all-done = f32[256,1,192]{2,1,0:T(1,128)S(1)} async-done(((f32[256,1,192]{2,1,0:T(1,128)}), f32[256,1,192]{2,1,0:T(1,128)S(1)}, u32[]{:S(2)}, u32[]{:S(2)}) %all-to-all-start) | async-done | bytes 196640 | tf_op jit(solution)/shard_map/while/body/eval_jaxpr/all_to_all | solution.py:126
  297.3 5.2 %all-to-all-start = ((f32[256,1,192]{2,1,0:T(1,128)}), f32[256,1,192]{2,1,0:T(1,128)S(1)}, u32[]{:S(2)}, u32[]{:S(2)}) async-start(f32[256,1,192]{2,1,0:T(1,128)} %reshape.430), calls=%async_computation | async-start | bytes 524288 | tf_op jit(solution)/shard_map/while/body/eval_jaxpr/all_to_all | solution.py:126
  302.5 15.3 %all-to-all-done = f32[256,1,192]{2,1,0:T(1,128)S(1)} async-done(((f32[256,1,192]{2,1,0:T(1,128)}), f32[256,1,192]{2,1,0:T(1,128)S(1)}, u32[]{:S(2)}, u32[]{:S(2)}) %all-to-all-start) | async-done | bytes 196640 | tf_op jit(solution)/shard_map/while/body/eval_jaxpr/all_to_all | solution.py:126
  330.8 5.2 %all-to-all-start = ((f32[256,1,192]{2,1,0:T(1,128)}), f32[256,1,192]{2,1,0:T(1,128)S(1)}, u32[]{:S(2)}, u32[]{:S(2)}) async-start(f32[256,1,192]{2,1,0:T(1,128)} %reshape.430), calls=%async_computation | async-start | bytes 524288 | tf_op jit(solution)/shard_map/while/body/eval_jaxpr/all_to_all | solution.py:126
  336.0 15.3 %all-to-all-done = f32[256,1,192]{2,1,0:T(1,128)S(1)} async-done(((f32[256,1,192]{2,1,0:T(1,128)}), f32[256,1,192]{2,1,0:T(1,128)S(1)}, u32[]{:S(2)}, u32[]{:S(2)}) %all-to-all-start) | async-done | bytes 196640 | tf_op jit(solution)/shard_map/while/body/eval_jaxpr/all_to_all | solution.py:126
  364.3 5.2 %all-to-all-start = ((f32[256,1,192]{2,1,0:T(1,128)}), f32[256,1,192]{2,1,0:T(1,128)S(1)}, u32[]{:S(2)}, u32[]{:S(2)}) async-start(f32[256,1,192]{2,1,0:T(1,128)} %reshape.430), calls=%async_computation | async-start | bytes 524288 | tf_op jit(solution)/shard_map/while/body/eval_jaxpr/all_to_all | solution.py:126
  369.5 15.3 %all-to-all-done = f32[256,1,192]{2,1,0:T(1,128)S(1)} async-done(((f32[256,1,192]{2,1,0:T(1,128)}), f32[256,1,192]{2,1,0:T(1,128)S(1)}, u32[]{:S(2)}, u32[]{:S(2)}) %all-to-all-start) | async-done | bytes 196640 | tf_op jit(solution)/shard_map/while/body/eval_jaxpr/all_to_all | solution.py:126
  396.5 10.6 %convolution_add_fusion = f32[3,8,8,6400]{3,2,1,0:T(8,128)S(1)} fusion(f32[3,8,8,320]{3,2,1,0:T(8,128)S(1)} %copy.44, f32[80,6400]{1,0:T(8,128)} %get-tuple-element.132, f32[80,6400]{1,0:T(8,128)} %get-tuple-element.131, f32[80,6400]{1,0:T(8,128)S(1)} %scatter-add.31, f32[80,6400]{1,0:T(8,128)} %scatter-add.24, f32[6400]{0:T(1024)S(1)} %multiply_multiply_fusion, ...), kind=kOutput, calls=%fused_computation.10 | convolution fusion | flops 4727193600 | bytes 13379328 | tf_op jit(solution)/shard_map/dot_general | solution.py:75
  407.2 5.3 %fusion.48 = (f32[3,8,8,6399]{3,2,1,0:T(8,128)}, f32[3,8,8,6399]{3,2,1,0:T(8,128)}) fusion(f32[3,8,8,6400]{3,2,1,0:T(8,128)S(1)} %convolution_add_fusion), kind=kLoop, calls=%fused_computation.116 | loop fusion | bytes 19657728 | tf_op jit(solution)/shard_map/slice | solution.py:51
  419.0 5.5 %fusion.50 = (f32[3,8,8,6320]{3,2,1,0:T(8,128)}, f32[3,8,8,6320]{3,2,1,0:T(8,128)}) fusion(f32[3,8,8,6400]{3,2,1,0:T(8,128)S(1)} %convolution_add_fusion), kind=kLoop, calls=%fused_computation.118 | loop fusion | bytes 19415040 | tf_op jit(solution)/shard_map/slice | solution.py:56
  425.8 10.9 %fusion.12 = (f32[3,8,8,6400]{3,2,1,0:T(8,128)S(1)}, f32[3,8,8,6400]{3,2,1,0:T(8,128)S(1)}, f32[3,8,8,6400]{3,2,1,0:T(8,128)}) fusion(f32[3,8,8,6400]{3,2,1,0:T(8,128)S(1)} %convolution_add_fusion, f32[3,8,8,1]{3,2,1,0:T(8,128)S(1)} %get-tuple-element.120, f32[3,8,8,6399]{3,2,1,0:T(8,128)} %get-tuple-element.122, f32[3,8,8,6399]{3,2,1,0:T(8,128)} %get-tuple-element.121, ...), kind=kLoop, calls=%fused_computation.26 | loop fusion | flops 19660800 | bytes 40576000 | tf_op jit(solution)/shard_map/mul | solution.py:52
  (137 shorter events, 84.3 us)
Async XLA Ops:
  2.4 13.6 %copy-start.12 = (s32[2]{0:T(128)S(1)}, s32[2]{0:T(128)}, u32[]{:S(2)}) copy-start(s32[2]{0:T(128)} %constant.172) | copy-start | bytes 28
  2.4 13.7 %copy-start.11 = (s32[2]{0:T(128)S(1)}, s32[2]{0:T(128)}, u32[]{:S(2)}) copy-start(s32[2]{0:T(128)} %constant.175) | copy-start | bytes 28
  2.4 13.9 %copy-start.6 = (s32[2048,4]{0,1:T(4,128)S(1)}, s32[2048,4]{0,1:T(4,128)}, u32[]{:S(2)}) copy-start(s32[2048,4]{0,1:T(4,128)} %param.22) | copy-start | bytes 98308
  14.7 7.9 %copy-start.10 = (f32[3,8]{1,0:T(4,128)S(1)}, f32[3,8]{1,0:T(4,128)}, u32[]{:S(2)}) copy-start(f32[3,8]{1,0:T(4,128)} %param.27) | copy-start | bytes 292
  16.7 51.4 %copy-start.7 = (f32[3,2048]{1,0:T(4,128)S(1)}, f32[3,2048]{1,0:T(4,128)}, u32[]{:S(2)}) copy-start(f32[3,2048]{1,0:T(4,128)} %param.19) | copy-start | bytes 73732
  17.3 51.1 %copy-start.8 = (f32[2048,4]{0,1:T(4,128)S(1)}, f32[2048,4]{0,1:T(4,128)}, u32[]{:S(2)}) copy-start(f32[2048,4]{0,1:T(4,128)} %param.20) | copy-start | bytes 98308
  17.6 1.3 copy-start.3
  22.5 45.6 %copy-start.1 = (f32[80,6400]{1,0:T(8,128)}, f32[80,6400]{1,0:T(8,128)S(1)}, u32[]{:S(2)}) copy-start(f32[80,6400]{1,0:T(8,128)S(1)} %scatter-add.30) | copy-start | bytes 6144004
  56.0 53.3 %all-to-all-start.1 = ((s32[32,1,512]{2,1,0:T(1,128)}), s32[32,1,512]{2,1,0:T(1,128)S(1)}, u32[]{:S(2)}, u32[]{:S(2)}) async-start(s32[32,1,512]{2,1,0:T(1,128)} %bitcast.2), calls=%async_computation.1 | async-start | bytes 131072 | tf_op jit(solution)/shard_map/all_to_all | solution.py:114
  100.7 6.1 %copy-start.9 = (f32[3,64]{1,0:T(4,128)S(1)}, f32[3,64]{1,0:T(4,128)}, u32[]{:S(2)}) copy-start(f32[3,64]{1,0:T(4,128)} %param.23) | copy-start | bytes 2308
  100.7 6.2 %copy-start.4 = (f32[6,64]{1,0:T(8,128)S(1)}, f32[6,64]{1,0:T(8,128)}, u32[]{:S(2)}) copy-start(f32[6,64]{1,0:T(8,128)} %param.24) | copy-start | bytes 4612
  100.7 7.9 %copy-start.2 = (f32[80,6400]{1,0:T(8,128)S(1)}, f32[80,6400]{1,0:T(8,128)}, u32[]{:S(2)}) copy-start(f32[80,6400]{1,0:T(8,128)} %copy-done.1) | copy-start | bytes 6144004
  100.7 8.5 %copy-start.13 = (f32[64]{0:T(128)S(1)}, f32[64]{0:T(128)}, u32[]{:S(2)}) copy-start(f32[64]{0:T(128)} %param.25) | copy-start | bytes 772
  109.2 18.7 %all-to-all-start.2 = ((f32[32,3,512]{2,1,0:T(4,128)}), f32[32,3,512]{2,1,0:T(4,128)S(1)}, u32[]{:S(2)}, u32[]{:S(2)}) async-start(f32[32,3,512]{2,1,0:T(4,128)} %bitcast.8), calls=%async_computation.2 | async-start | bytes 524288 | tf_op jit(solution)/shard_map/all_to_all | solution.py:113
  241.7 5.4 %copy-start.5 = (s32[6,64]{1,0:T(8,128)S(1)}, s32[6,64]{1,0:T(8,128)}, u32[]{:S(2)}) copy-start(s32[6,64]{1,0:T(8,128)} %param.26) | copy-start | bytes 4612
  248.5 35.8 %all-to-all-start = ((f32[256,1,192]{2,1,0:T(1,128)}), f32[256,1,192]{2,1,0:T(1,128)S(1)}, u32[]{:S(2)}, u32[]{:S(2)}) async-start(f32[256,1,192]{2,1,0:T(1,128)} %reshape.430), calls=%async_computation | async-start | bytes 524288 | tf_op jit(solution)/shard_map/while/body/eval_jaxpr/all_to_all | solution.py:126
  297.3 20.6 %all-to-all-start = ((f32[256,1,192]{2,1,0:T(1,128)}), f32[256,1,192]{2,1,0:T(1,128)S(1)}, u32[]{:S(2)}, u32[]{:S(2)}) async-start(f32[256,1,192]{2,1,0:T(1,128)} %reshape.430), calls=%async_computation | async-start | bytes 524288 | tf_op jit(solution)/shard_map/while/body/eval_jaxpr/all_to_all | solution.py:126
  330.8 20.6 %all-to-all-start = ((f32[256,1,192]{2,1,0:T(1,128)}), f32[256,1,192]{2,1,0:T(1,128)S(1)}, u32[]{:S(2)}, u32[]{:S(2)}) async-start(f32[256,1,192]{2,1,0:T(1,128)} %reshape.430), calls=%async_computation | async-start | bytes 524288 | tf_op jit(solution)/shard_map/while/body/eval_jaxpr/all_to_all | solution.py:126
  364.3 20.6 %all-to-all-start = ((f32[256,1,192]{2,1,0:T(1,128)}), f32[256,1,192]{2,1,0:T(1,128)S(1)}, u32[]{:S(2)}, u32[]{:S(2)}) async-start(f32[256,1,192]{2,1,0:T(1,128)} %reshape.430), calls=%async_computation | async-start | bytes 524288 | tf_op jit(solution)/shard_map/while/body/eval_jaxpr/all_to_all | solution.py:126
  407.1 18.7 %copy-start = (f32[3,8,8,6400]{3,2,1,0:T(8,128)}, f32[3,8,8,6400]{3,2,1,0:T(8,128)S(1)}, u32[]{:S(2)}) copy-start(f32[3,8,8,6400]{3,2,1,0:T(8,128)S(1)} %convolution_add_fusion) | copy-start | bytes 14745604
  413.2 11.5 %collective-permute-start = (f32[3,8,1,6400]{3,2,1,0:T(1,128)S(1)}, f32[3,8,1,6400]{3,2,1,0:T(1,128)S(1)}, u32[]{:S(2)}, u32[]{:S(2)}) collective-permute-start(f32[3,8,1,6400]{3,2,1,0:T(1,128)S(1)} %get-tuple-element.127), channel_id=1, source_target_pairs={{1,0},{2,1},{3,2},{4,3},{5,4},{6,5},{7,6},{9,8},{10,9},{11,10},{12... | collective-permute-start | bytes 1843208 | tf_op jit(solution)/shard_map/ppermute | solution.py:20
  415.1 10.7 %collective-permute-start.1 = (f32[3,8,1,6400]{3,2,1,0:T(1,128)S(1)}, f32[3,8,1,6400]{3,2,1,0:T(1,128)S(1)}, u32[]{:S(2)}, u32[]{:S(2)}) collective-permute-start(f32[3,8,1,6400]{3,2,1,0:T(1,128)S(1)} %get-tuple-element.128), channel_id=1, source_target_pairs={{0,1},{1,2},{2,3},{3,4},{4,5},{5,6},{6,7},{8,9},{9,10},{10,11},{11... | collective-permute-start | bytes 1843208 | tf_op jit(solution)/shard_map/ppermute | solution.py:17
